TPU v7x, 256 devices: a whole 4x4x8 slice. The times are simulated.
256 devices in a mesh: gen: 32 (over z, y_lo, core), neur: 4 (over x), box: 2 (over y_hi).
Axes of the slice: x: 4, y: 4 (y_hi: 2, y_lo: 2; y = y_hi * 2 + y_lo), z: 8, core: 2. Of those that a mesh axis runs over, the one named last changes fastest.
Arguments:
- gens: bfloat16 [8, 1024, 4096], P('box', 'gen'), may hold values from -1 to 1
- center: bfloat16 [8, 4096], P('box'), may hold values from -6 to 6
- weight: bfloat16 [4096, 2048], P('gen', 'neur'), may hold values from -0.09375 to 0.09375
- bias: float32 [2048], P('neur'), may hold values from -3 to 3
- phase: int32 [8, 2048], P('box', 'neur'), may hold values from 0 to 2
- gens_cot: bfloat16 [8, 1024, 2048], P('box', 'gen', 'neur'), may hold values from -6 to 6
- center_cot: float32 [8, 2048], P('box', 'neur'), may hold values from -6 to 6
- offset_cot: float32 [8, 2048], P('box', 'neur'), may hold values from -6 to 6
Outputs:
- center_out: float32 [8, 2048], P('box', 'neur')
- gens_out: bfloat16 [8, 1024, 2048], P('box', 'gen', 'neur')
- offset: float32 [8, 2048], P('box', 'neur')
- weight_grad: float32 [4096, 2048], P('gen', 'neur')
- bias_grad: float32 [2048], P('neur')
- gens_grad: float32 [8, 1024, 4096], P('box', 'gen', 'neur')
- center_grad: float32 [8, 4096], P('box', 'neur')
Inputs may be any that keep to these rules, and one draw needn't show every extreme that they name: `phase`: 0 marks an inactive neuron, 1 an active one, 2 one that crosses zero.
All inputs are finite; a program needn't handle non-finite values.
Results may differ from a plain program's by a relative error of at most 0.006.
Values may be sent and summed in bfloat16 or wider, within the bound.
A program may use at most 64 MiB of HBM per device.

v0:
```python
import jax
import jax.numpy as jnp
from jax import lax
from jax.sharding import PartitionSpec as P


def neuron(center_pre, radius, phase):
    upper = center_pre + radius
    lower = center_pre - radius
    ratio = jnp.clip(upper / (upper - lower + 1e-05), 0.0, 1.0)
    active = (phase == 1).astype(center_pre.dtype)
    crossing = (phase == 2).astype(center_pre.dtype)
    slope = active + crossing * ratio
    offset = crossing * (-ratio * lower * 0.5)
    return (slope, slope * center_pre + offset, offset)


def body(gens, center, weight, bias, phase, gens_cot, center_cot, offset_cot):
    box_dev, gen_dev, width = gens.shape
    local_cols = weight.shape[1]
    local_rows = box_dev * gen_dev
    wide = jnp.concatenate([gens.reshape(local_rows, width), center], 0)
    full_weight = lax.all_gather(weight, "gen", axis=0, tiled=True)
    product = jnp.dot(wide, full_weight, preferred_element_type=jnp.float32)
    gen_pre = product[:local_rows].reshape(box_dev, gen_dev, local_cols)
    center_pre = product[local_rows:] + bias
    part_radius = jnp.sum(jnp.abs(gen_pre), axis=1)
    cot_wide = gens_cot.astype(jnp.float32)
    radius = lax.psum(part_radius, "gen")
    slope, center_out, offset = neuron(center_pre, radius, phase)
    gens_out = (slope[:, None, :] * gen_pre).astype(jnp.bfloat16)
    intersection = lax.psum(jnp.sum(cot_wide * gen_pre, axis=1), "gen")
    unused, pull = jax.vjp(lambda a, b: neuron(a, b, phase), center_pre, radius)
    g_center, g_radius = pull((intersection, center_cot, offset_cot))
    gen_back = (slope[:, None, :] * cot_wide + jnp.sign(gen_pre) * g_radius[:, None, :]).astype(
        jnp.bfloat16
    )
    center_back = g_center.astype(jnp.bfloat16)
    back = jnp.concatenate([gen_back.reshape(local_rows, local_cols), center_back], 0)
    first_gen = (lax.axis_index("gen") == 0).astype(jnp.bfloat16)
    back_owned = jnp.concatenate(
        [gen_back.reshape(local_rows, local_cols), center_back * first_gen], 0
    )
    bias_part = jnp.sum(g_center, axis=0)
    shares = lax.psum_scatter(
        lax.dot_general(
            wide, back_owned, (((0,), (0,)), ((), ())), preferred_element_type=jnp.float32
        ),
        "gen",
        scatter_dimension=0,
        tiled=True,
    )
    weight_grad, bias_grad = lax.psum((shares, bias_part), "box")
    partial_back = lax.dot_general(
        back, full_weight, (((1,), (1,)), ((), ())), preferred_element_type=jnp.float32
    )
    summed = lax.psum_scatter(partial_back, "neur", scatter_dimension=1, tiled=True)
    gens_grad = summed[:local_rows].reshape(box_dev, gen_dev, summed.shape[1])
    center_grad = summed[local_rows:]
    return (center_out, gens_out, offset, weight_grad, bias_grad, gens_grad, center_grad)


def solution(mesh):
    return jax.shard_map(
        body,
        mesh=mesh,
        in_specs=(
            P("box", "gen", None),
            P("box", None),
            P("gen", "neur"),
            P("neur"),
            P("box", "neur"),
            P("box", "gen", "neur"),
            P("box", "neur"),
            P("box", "neur"),
        ),
        out_specs=(
            P("box", "neur"),
            P("box", "gen", "neur"),
            P("box", "neur"),
            P("gen", "neur"),
            P("neur"),
            P("box", "gen", "neur"),
            P("box", "neur"),
        ),
        check_vma=False,
    )
```

profile of v0, /device:TPU:1, one launch (start us, length us, event | category | flops | bytes accessed | tf_op | source)
XLA Modules:
  0.0 407.0 jit_solution(1934625204832896701)
XLA Ops:
  7.2 0.0 all-gather.2.cloned.1.call-start
  7.2 0.7 all-gather.2.cloned.1.call-update
  7.9 0.0 reduce-scatter.3.cloned.1.call-start
  8.0 72.6 %all-gather.2.cloned.1.call-done = bf16[4096,512]{1,0:T(8,128)(2,1)} async-done(((bf16[128,512]{1,0:T(8,128)(2,1)}), bf16[4096,512]{1,0:T(8,128)(2,1)}) %all-gather.2.cloned.1.call-update) | async-done | bytes 4194320 | tf_op jit(solution)/shard_map/all_gather | solution.py:23
  80.6 0.0 copy-start.1
  80.6 0.0 copy-start.3
  80.6 0.0 copy-start.4
  80.6 0.0 copy-start.5
  80.6 0.0 copy-start.6
  80.6 0.0 copy-start
  80.6 0.0 copy-start.2
  80.6 3.4 fusion.1
  84.0 0.0 copy-done.1
  84.0 0.1 fusion.4
  84.1 101.8 %all-reduce = (f32[4,512]{1,0:T(4,128)S(1)}, f32[4,512]{1,0:T(4,128)S(1)}) all-reduce(f32[4,512]{1,0:T(4,128)S(1)} %get-tuple-element.8, f32[4,512]{1,0:T(4,128)S(1)} %get-tuple-element.7), channel_id=1, replica_groups=mesh['gen'=32,'neur'=4,'box'=2] {'gen'}, use_global_device_ids=true, to_apply=%region_1.0 | all-reduce | flops 4096 | bytes 32768 | tf_op jit(solution)/shard_map/psum | solution.py:29
  185.9 0.0 copy-done.3
  185.9 0.0 copy-done.4
  185.9 0.0 copy-done.5
  185.9 0.0 copy-done.6
  186.0 0.8 fusion.3
  186.8 0.0 copy-done
  186.8 0.0 copy-done.2
  186.8 4.6 %fusion = f32[4096,512]{1,0:T(8,128)} fusion(bf16[4,4096]{1,0:T(4,128)(2,1)S(1)} %copy-done.2, bf16[128,4096]{1,0:T(8,128)(2,1)S(1)} %bitcast.13, bf16[4,512]{1,0:T(4,128)(2,1)S(1)} %get-tuple-element.16, bf16[128,512]{1,0:T(8,128)(2,1)S(1)} %bitcast.10), kind=kOutput, calls=%fused_computation.1 | convolution fusion | flops 556081152 | bytes 9605120 | tf_op jit(solution)/shard_map/dot_general | solution.py:46
  191.3 0.0 reduce-scatter.3.cloned.1.call-update
  191.4 0.0 reduce-scatter.5.cloned.1.call-start
  191.4 5.1 %fusion.7 = f32[132,4096]{1,0:T(8,128)} fusion(bf16[4096,512]{1,0:T(8,128)(2,1)} %all-gather.2.cloned.1.call-done, bf16[4,512]{1,0:T(4,128)(2,1)S(1)} %get-tuple-element.17, bf16[128,512]{1,0:T(8,128)(2,1)S(1)} %bitcast.11), kind=kOutput, calls=%fused_computation.12 | convolution fusion | flops 553918464 | bytes 6492160 | tf_op jit(solution)/shard_map/dot_general | solution.py:54
  196.5 0.0 reduce-scatter.5.cloned.1.call-update
  196.5 0.0 all-reduce.3.cloned.1.call-start
  196.5 126.5 %reduce-scatter.3.cloned.1.call-done = f32[128,512]{1,0:T(8,128)} async-done(((f32[4096,512]{1,0:T(8,128)}), f32[128,512]{1,0:T(8,128)}) %reduce-scatter.3.cloned.1.call-update) | async-done | bytes 262160 | tf_op jit(solution)/shard_map/reduce_scatter | solution.py:45
  323.1 0.0 all-reduce.3.cloned.1.call-update
  323.1 5.9 %psum.31 = f32[512]{0:T(512)} all-reduce(f32[512]{0:T(512)S(1)} %get-tuple-element.11), channel_id=1, replica_groups=mesh['gen'=32,'neur'=4,'box'=2] {'box'}, use_global_device_ids=true, to_apply=%region_7.8 | all-reduce | flops 512 | bytes 4096 | tf_op jit(solution)/shard_map/psum | solution.py:53
  328.9 0.6 multiply_add_fusion.1
  329.6 30.9 %reduce-scatter.5.cloned.1.call-done = f32[132,1024]{1,0:T(8,128)} async-done(((f32[132,4096]{1,0:T(8,128)}), f32[132,1024]{1,0:T(8,128)}) %reduce-scatter.5.cloned.1.call-update) | async-done | bytes 540688 | tf_op jit(solution)/shard_map/reduce_scatter | solution.py:57
  360.5 1.4 slice.19
  361.9 1.9 slice.18
  363.7 35.1 %all-reduce.3.cloned.1.call-done = f32[128,512]{1,0:T(8,128)} async-done(((f32[128,512]{1,0:T(8,128)}), f32[128,512]{1,0:T(8,128)}) %all-reduce.3.cloned.1.call-update) | async-done | bytes 262160 | tf_op jit(solution)/shard_map/psum | solution.py:53
  398.8 1.7 copy.16
  (4 shorter events, 0.1 us)
Async XLA Ops:
  7.2 73.4 %all-gather.2.cloned.1.call-start = ((), (), s32[]{:S(2)}) async-start(), calls=%async_computation.2 | async-start | bytes 4325376 | tf_op jit(solution)/shard_map/all_gather | solution.py:23
  7.9 315.1 %reduce-scatter.3.cloned.1.call-start = ((), (), s32[]{:S(2)}) async-start(), calls=%async_computation.3 | async-start | bytes 8650752 | tf_op jit(solution)/shard_map/reduce_scatter | solution.py:45
  80.6 3.4 copy-start.1
  80.6 105.3 %copy-start.3 = (f32[4,512]{1,0:T(4,128)S(1)}, f32[4,512]{1,0:T(4,128)}, u32[]{:S(2)}) copy-start(f32[4,512]{1,0:T(4,128)} %param.14) | copy-start | bytes 24580
  80.6 105.3 %copy-start.4 = (f32[4,512]{1,0:T(4,128)S(1)}, f32[4,512]{1,0:T(4,128)}, u32[]{:S(2)}) copy-start(f32[4,512]{1,0:T(4,128)} %param.15) | copy-start | bytes 24580
  80.6 105.3 %copy-start.5 = (s32[4,512]{1,0:T(4,128)S(1)}, s32[4,512]{1,0:T(4,128)}, u32[]{:S(2)}) copy-start(s32[4,512]{1,0:T(4,128)} %param.12) | copy-start | bytes 24580
  80.6 105.3 %copy-start.6 = (f32[512]{0:T(512)S(1)}, f32[512]{0:T(512)}, u32[]{:S(2)}) copy-start(f32[512]{0:T(512)} %param.11) | copy-start | bytes 6148
  80.6 106.2 %copy-start = (bf16[4,32,4096]{2,1,0:T(8,128)(2,1)S(1)}, bf16[4,32,4096]{2,1,0:T(8,128)(2,1)}, u32[]{:S(2)}) copy-start(bf16[4,32,4096]{2,1,0:T(8,128)(2,1)} %param.8) | copy-start | bytes 3145732
  80.6 106.2 %copy-start.2 = (bf16[4,4096]{1,0:T(4,128)(2,1)S(1)}, bf16[4,4096]{1,0:T(4,128)(2,1)}, u32[]{:S(2)}) copy-start(bf16[4,4096]{1,0:T(4,128)(2,1)} %param.9) | copy-start | bytes 98308
  191.4 169.1 %reduce-scatter.5.cloned.1.call-start = ((), (), s32[]{:S(2)}) async-start(), calls=%async_computation.5 | async-start | bytes 2785280 | tf_op jit(solution)/shard_map/reduce_scatter | solution.py:57
  196.5 202.3 %all-reduce.3.cloned.1.call-start = ((), (), s32[]{:S(2)}) async-start(), calls=%async_computation.4 | async-start | bytes 524288 | tf_op jit(solution)/shard_map/psum | solution.py:53
Sparse Core Ops, SparseCore 0:
  9.8 70.6 all-gather.1
  191.5 131.5 reduce-scatter.2
  325.6 34.8 reduce-scatter.4
  362.9 35.8 all-reduce.2
where the time goes:
time: 407 us
  waiting for transfers between devices  266 us (65%)
  blocking collectives  108 us (27%)
  between operations  13.9 us (3%)
  matrix products  13 us (3%)
  local copies, waits for them, and re-layouts  4.95 us (1%)
    reduce_scatter x1, waiting for transfers between devices, body(): lax.psum_scatter(lax.dot_general(wide, back_owned, (((0,), (0,)), ((), ()...  127 us
    psum x1, blocking collectives, body(): radius = lax.psum(part_radius, 'gen')  102 us
    all_gather x1, waiting for transfers between devices, body(): full_weight = lax.all_gather(weight, 'gen', axis=0, tiled=True)  72.6 us
    psum x1, waiting for transfers between devices, body(): weight_grad, bias_grad = lax.psum((shares, bias_part), 'box')  35.1 us
    reduce_scatter x1, waiting for transfers between devices, body(): lax.psum_scatter(partial_back, 'neur', scatter_dimension=1, tiled=True)  30.9 us
  transfers between devices with their start and end apart: 4, of which 4 were waited for; matrix products, arithmetic and copies ran while one was open for 2% of the time, Pallas kernels for 0%

commit v1 on v0

--- a/solution.py
+++ b/solution.py
@@ -26,7 +26,7 @@
     center_pre = product[local_rows:] + bias
     part_radius = jnp.sum(jnp.abs(gen_pre), axis=1)
     cot_wide = gens_cot.astype(jnp.float32)
-    radius = lax.psum(part_radius, "gen")
+    radius = jnp.sum(lax.all_gather(part_radius, "gen"), axis=0)
     slope, center_out, offset = neuron(center_pre, radius, phase)
     gens_out = (slope[:, None, :] * gen_pre).astype(jnp.bfloat16)
     intersection = lax.psum(jnp.sum(cot_wide * gen_pre, axis=1), "gen")

time: 407 us -> 389 us (0.956)
  blocking collectives: 108 us -> 92.8 us
    psum x1, blocking collectives: 102 us -> 53.7 us  [body(): intersection = lax.psum(jnp.sum(cot_wide * gen_pre, axis=1), 'gen')]
    all_gather x0 -> x1, blocking collectives: none -> 33.2 us  [body(): radius = jnp.sum(lax.all_gather(part_radius, 'gen'), axis=0)]
where the time goes in v1:
time: 389 us; the launch traced here: 388 us
  waiting for transfers between devices  262 us (67%)
  blocking collectives  92.8 us (24%)
  between operations  13.9 us (4%)
  matrix products  12.9 us (3%)
  local copies, waits for them, and re-layouts  4.95 us (1%)
    reduce_scatter x1, waiting for transfers between devices, body(): lax.psum_scatter(lax.dot_general(wide, back_owned, (((0,), (0,)), ((), ()...  123 us
    all_gather x1, waiting for transfers between devices, body(): full_weight = lax.all_gather(weight, 'gen', axis=0, tiled=True)  72.6 us
    psum x1, blocking collectives, body(): intersection = lax.psum(jnp.sum(cot_wide * gen_pre, axis=1), 'gen')  53.7 us
    psum x1, waiting for transfers between devices, body(): weight_grad, bias_grad = lax.psum((shares, bias_part), 'box')  35 us
    all_gather x1, blocking collectives, body(): radius = jnp.sum(lax.all_gather(part_radius, 'gen'), axis=0)  33.2 us
    reduce_scatter x1, waiting for transfers between devices, body(): lax.psum_scatter(partial_back, 'neur', scatter_dimension=1, tiled=True)  31.2 us
  transfers between devices with their start and end apart: 4, of which 4 were waited for; matrix products, arithmetic and copies ran while one was open for 2% of the time, Pallas kernels for 0%

profile of v1, /device:TPU:1, one launch (start us, length us, event | category | flops | bytes accessed | tf_op | source)
XLA Modules:
  0.0 388.5 jit_solution(7551191972071794625)
XLA Ops:
  7.2 0.0 all-gather.4.cloned.1.call-start
  7.2 0.7 all-gather.4.cloned.1.call-update
  7.9 0.0 reduce-scatter.3.cloned.1.call-start
  8.0 72.6 %all-gather.4.cloned.1.call-done = bf16[4096,512]{1,0:T(8,128)(2,1)} async-done(((bf16[128,512]{1,0:T(8,128)(2,1)}), bf16[4096,512]{1,0:T(8,128)(2,1)}) %all-gather.4.cloned.1.call-update) | async-done | bytes 4194320 | tf_op jit(solution)/shard_map/all_gather | solution.py:23
  80.6 0.0 copy-start.1
  80.6 0.0 copy-start.3
  80.6 0.0 copy-start.4
  80.6 0.0 copy-start.5
  80.6 0.0 copy-start.6
  80.6 0.0 copy-start.2
  80.6 3.3 fusion.1
  83.9 0.0 copy-done.1
  83.9 0.0 copy-start
  83.9 0.1 fusion.4
  84.0 53.7 %psum.21 = f32[4,512]{1,0:T(4,128)S(1)} all-reduce(f32[4,512]{1,0:T(4,128)S(1)} %get-tuple-element.7), channel_id=1, replica_groups=mesh['gen'=32,'neur'=4,'box'=2] {'gen'}, use_global_device_ids=true, to_apply=%region_3.4 | all-reduce | flops 2048 | bytes 16384 | tf_op jit(solution)/shard_map/psum | solution.py:32
  137.8 33.2 %all-gather.1 = f32[32,4,512]{2,1,0:T(4,128)S(1)} all-gather(f32[1,4,512]{2,1,0:T(4,128)S(1)} %bitcast.16), channel_id=2, replica_groups=mesh['gen'=32,'neur'=4,'box'=2] {'gen'}, dimensions={0}, use_global_device_ids=true | all-gather | bytes 270336 | tf_op jit(solution)/shard_map/all_gather | solution.py:29
  171.0 0.1 reduce_sum.37
  171.0 0.0 copy-done.3
  171.0 0.0 copy-done.4
  171.0 0.0 copy-done.5
  171.0 0.0 copy-done.6
  171.2 0.8 fusion.3
  171.9 0.0 copy-done.2
  171.9 0.0 copy-done
  171.9 4.6 %fusion = f32[4096,512]{1,0:T(8,128)} fusion(bf16[4,4096]{1,0:T(4,128)(2,1)S(1)} %copy-done.2, bf16[128,4096]{1,0:T(8,128)(2,1)S(1)} %bitcast.14, bf16[4,512]{1,0:T(4,128)(2,1)S(1)} %get-tuple-element.14, bf16[128,512]{1,0:T(8,128)(2,1)S(1)} %bitcast.11), kind=kOutput, calls=%fused_computation.1 | convolution fusion | flops 556081152 | bytes 9605120 | tf_op jit(solution)/shard_map/dot_general | solution.py:46
  176.5 0.0 reduce-scatter.3.cloned.1.call-update
  176.5 0.0 reduce-scatter.5.cloned.1.call-start
  176.6 5.1 %fusion.7 = f32[132,4096]{1,0:T(8,128)} fusion(bf16[4096,512]{1,0:T(8,128)(2,1)} %all-gather.4.cloned.1.call-done, bf16[4,512]{1,0:T(4,128)(2,1)S(1)} %get-tuple-element.15, bf16[128,512]{1,0:T(8,128)(2,1)S(1)} %bitcast.12), kind=kOutput, calls=%fused_computation.12 | convolution fusion | flops 553918464 | bytes 6492160 | tf_op jit(solution)/shard_map/dot_general | solution.py:54
  181.6 0.0 reduce-scatter.5.cloned.1.call-update
  181.7 0.0 all-reduce.2.cloned.1.call-start
  181.7 122.5 %reduce-scatter.3.cloned.1.call-done = f32[128,512]{1,0:T(8,128)} async-done(((f32[4096,512]{1,0:T(8,128)}), f32[128,512]{1,0:T(8,128)}) %reduce-scatter.3.cloned.1.call-update) | async-done | bytes 262160 | tf_op jit(solution)/shard_map/reduce_scatter | solution.py:45
  304.2 0.0 all-reduce.2.cloned.1.call-update
  304.3 5.9 %psum.23 = f32[512]{0:T(512)} all-reduce(f32[512]{0:T(512)S(1)} %get-tuple-element.9), channel_id=1, replica_groups=mesh['gen'=32,'neur'=4,'box'=2] {'box'}, use_global_device_ids=true, to_apply=%region_7.8 | all-reduce | flops 512 | bytes 4096 | tf_op jit(solution)/shard_map/psum | solution.py:53
  310.1 0.6 multiply_add_fusion.1
  310.7 31.2 %reduce-scatter.5.cloned.1.call-done = f32[132,1024]{1,0:T(8,128)} async-done(((f32[132,4096]{1,0:T(8,128)}), f32[132,1024]{1,0:T(8,128)}) %reduce-scatter.5.cloned.1.call-update) | async-done | bytes 540688 | tf_op jit(solution)/shard_map/reduce_scatter | solution.py:57
  342.0 1.4 slice.19
  343.3 1.9 slice.18
  345.2 35.0 %all-reduce.2.cloned.1.call-done = f32[128,512]{1,0:T(8,128)} async-done(((f32[128,512]{1,0:T(8,128)}), f32[128,512]{1,0:T(8,128)}) %all-reduce.2.cloned.1.call-update) | async-done | bytes 262160 | tf_op jit(solution)/shard_map/psum | solution.py:53
  380.3 1.7 copy.16
  (4 shorter events, 0.1 us)
Async XLA Ops:
  7.2 73.4 %all-gather.4.cloned.1.call-start = ((), (), s32[]{:S(2)}) async-start(), calls=%async_computation.2 | async-start | bytes 4325376 | tf_op jit(solution)/shard_map/all_gather | solution.py:23
  7.9 296.3 %reduce-scatter.3.cloned.1.call-start = ((), (), s32[]{:S(2)}) async-start(), calls=%async_computation.3 | async-start | bytes 8650752 | tf_op jit(solution)/shard_map/reduce_scatter | solution.py:45
  80.6 3.3 copy-start.1
  80.6 90.5 %copy-start.3 = (f32[4,512]{1,0:T(4,128)S(1)}, f32[4,512]{1,0:T(4,128)}, u32[]{:S(2)}) copy-start(f32[4,512]{1,0:T(4,128)} %param.14) | copy-start | bytes 24580
  80.6 90.5 %copy-start.4 = (f32[4,512]{1,0:T(4,128)S(1)}, f32[4,512]{1,0:T(4,128)}, u32[]{:S(2)}) copy-start(f32[4,512]{1,0:T(4,128)} %param.15) | copy-start | bytes 24580
  80.6 90.5 %copy-start.5 = (s32[4,512]{1,0:T(4,128)S(1)}, s32[4,512]{1,0:T(4,128)}, u32[]{:S(2)}) copy-start(s32[4,512]{1,0:T(4,128)} %param.12) | copy-start | bytes 24580
  80.6 90.5 %copy-start.6 = (f32[512]{0:T(512)S(1)}, f32[512]{0:T(512)}, u32[]{:S(2)}) copy-start(f32[512]{0:T(512)} %param.11) | copy-start | bytes 6148
  80.6 91.4 %copy-start.2 = (bf16[4,4096]{1,0:T(4,128)(2,1)S(1)}, bf16[4,4096]{1,0:T(4,128)(2,1)}, u32[]{:S(2)}) copy-start(bf16[4,4096]{1,0:T(4,128)(2,1)} %param.9) | copy-start | bytes 98308
  83.9 88.0 %copy-start = (bf16[4,32,4096]{2,1,0:T(8,128)(2,1)S(1)}, bf16[4,32,4096]{2,1,0:T(8,128)(2,1)}, u32[]{:S(2)}) copy-start(bf16[4,32,4096]{2,1,0:T(8,128)(2,1)} %param.8) | copy-start | bytes 3145732
  176.5 165.4 %reduce-scatter.5.cloned.1.call-start = ((), (), s32[]{:S(2)}) async-start(), calls=%async_computation.5 | async-start | bytes 2785280 | tf_op jit(solution)/shard_map/reduce_scatter | solution.py:57
  181.7 198.6 %all-reduce.2.cloned.1.call-start = ((), (), s32[]{:S(2)}) async-start(), calls=%async_computation.4 | async-start | bytes 524288 | tf_op jit(solution)/shard_map/psum | solution.py:53
Sparse Core Ops, SparseCore 0:
  9.8 70.6 all-gather.3
  176.6 127.5 reduce-scatter.2
  306.8 35.0 reduce-scatter.4
  344.4 35.8 all-reduce.1
